TPU v7x, 256 devices: a whole 4x4x8 slice. The times are simulated.
256 devices in a mesh: grp: 16 (over z, core), ing: 16 (over y, x).
Axes of the slice: x: 4, y: 4, z: 8, core: 2. Of those that a mesh axis runs over, the one named last changes fastest.
Arguments:
- amplitudes: bfloat16 [512, 800, 800], P('grp', 'ing'), may hold values from -6 to 6
- integrals: bfloat16 [512, 800, 800], P('grp', 'ing'), may hold values from -0.0024414062 to 0.0024414062
- fock_block: bfloat16 [800, 800], P('ing'), may hold values from -0.625 to 0.625
- virtual_irrep: int32 [800], replicated, may hold values from 0 to 7, as said below
- pair_irrep: int32 [512], P(('grp', 'ing')), may hold values from 0 to 7
- pair_energy: float32 [512], P(('grp', 'ing')), may hold values from -4 to -1
- virtual_energy: float32 [800], replicated, may hold values from 0.5 to 4
Outputs:
- update: float32 [512, 800, 800], P('grp', 'ing')
Inputs may be any that keep to these rules, and one draw needn't show every extreme that they name: `virtual_irrep`: the orbitals of one irreducible representation form one contiguous run of 100 plus or minus at most 25 orbitals, and all 8 representations occur.
All inputs are finite; a program needn't handle non-finite values.
Results may differ from a plain program's by a relative error of at most 0.0029.
Values may be sent and summed in bfloat16 or wider, within the bound.
A program may use at most 128 MiB of HBM per device.

v0:
```python
import jax
import jax.numpy as jnp
from jax import lax
from jax.sharding import PartitionSpec as P


def symmetry_mask(values, pair_irrep, virtual_irrep):
    allowed = (
        jnp.bitwise_xor(virtual_irrep[:, None], virtual_irrep[None, :])[None]
        == pair_irrep[:, None, None]
    )
    return jnp.where(allowed, values, jnp.zeros_like(values))


def body(amplitudes, integrals, fock_block, virtual_irrep, pair_irrep, pair_energy, virtual_energy):
    same_irrep = virtual_irrep[:, None] == virtual_irrep[None, :]
    whole_amps, whole_ints = (
        lax.all_to_all(amplitudes, "ing", split_axis=0, concat_axis=1, tiled=True),
        lax.all_to_all(integrals, "ing", split_axis=0, concat_axis=1, tiled=True),
    )
    amp_masked = symmetry_mask(whole_amps, pair_irrep, virtual_irrep)
    int_masked = symmetry_mask(whole_ints, pair_irrep, virtual_irrep)
    partial_value = jnp.einsum(
        "paf,pef->ae", amp_masked, int_masked, preferred_element_type=jnp.float32
    )
    correction = lax.psum(partial_value, ("grp", "ing"))
    fock_full = lax.all_gather(fock_block, "ing", axis=0, tiled=True)
    fock_part = jnp.where(
        same_irrep, fock_full.astype(jnp.float32), jnp.zeros(fock_full.shape, jnp.float32)
    )
    operator_vv = (fock_part + correction).astype(jnp.bfloat16)
    product = jnp.einsum("pae,be->pab", amp_masked, operator_vv, preferred_element_type=jnp.float32)
    denominator = (
        pair_energy[:, None, None] - virtual_energy[None, :, None] - virtual_energy[None, None, :]
    )
    scaled = (product - jnp.swapaxes(product, 1, 2)) / denominator
    return lax.all_to_all(scaled, "ing", split_axis=1, concat_axis=0, tiled=True)


def solution(mesh):
    in_specs = (
        P("grp", "ing", None),
        P("grp", "ing", None),
        P("ing", None),
        P(),
        P(("grp", "ing")),
        P(("grp", "ing")),
        P(),
    )
    out_specs = P("grp", "ing", None)
    return jax.shard_map(body, mesh=mesh, in_specs=in_specs, out_specs=out_specs, check_vma=False)
```

profile of v0, /device:TPU:99, one launch (start us, length us, event | category | flops | bytes accessed | tf_op | source)
XLA Modules:
  0.0 516.4 jit_solution(2653213600742417975)
XLA Ops:
  7.4 4.4 copy.25
  11.8 6.9 %all-to-all-start = ((bf16[32,50,800]{2,1,0:T(8,128)(2,1)}), bf16[32,50,800]{2,1,0:T(8,128)(2,1)S(1)}, u32[]{:S(2)}, u32[]{:S(2)}) async-start(bf16[32,50,800]{2,1,0:T(8,128)(2,1)} %copy.25), calls=%async_computation | async-start | bytes 6422528 | tf_op jit(solution)/shard_map/all_to_all | solution.py:18
  18.7 4.5 copy.27
  23.2 0.0 copy-start.2
  23.2 39.1 %all-to-all-done = bf16[32,50,800]{2,1,0:T(8,128)(2,1)S(1)} async-done(((bf16[32,50,800]{2,1,0:T(8,128)(2,1)}), bf16[32,50,800]{2,1,0:T(8,128)(2,1)S(1)}, u32[]{:S(2)}, u32[]{:S(2)}) %all-to-all-start) | async-done | bytes 2560032 | tf_op jit(solution)/shard_map/all_to_all | solution.py:18
  62.3 8.3 %all-to-all-start.1 = ((bf16[32,50,800]{2,1,0:T(8,128)(2,1)}), bf16[32,50,800]{2,1,0:T(8,128)(2,1)}, u32[]{:S(2)}, u32[]{:S(2)}) async-start(bf16[32,50,800]{2,1,0:T(8,128)(2,1)} %copy.27), calls=%async_computation.1 | async-start | bytes 6422528 | tf_op jit(solution)/shard_map/all_to_all | solution.py:19
  70.7 0.0 all-gather.3.cloned.1.call-start
  70.7 0.7 all-gather.3.cloned.1.call-update
  71.4 0.0 all-reduce.2.cloned.1.call-start
  71.4 0.0 copy-done.2
  71.5 1.8 broadcast_xor_fusion
  73.3 3.8 copy.26
  77.1 35.5 %all-to-all-done.1 = bf16[32,50,800]{2,1,0:T(8,128)(2,1)} async-done(((bf16[32,50,800]{2,1,0:T(8,128)(2,1)}), bf16[32,50,800]{2,1,0:T(8,128)(2,1)}, u32[]{:S(2)}, u32[]{:S(2)}) %all-to-all-start.1) | async-done | bytes 2560032 | tf_op jit(solution)/shard_map/all_to_all | solution.py:19
  112.6 0.0 copy-start
  112.6 0.0 copy-start.1
  112.6 0.0 copy-start.4
  112.6 4.3 copy.28
  116.9 0.0 copy-done
  116.9 0.0 copy-done.1
  116.9 0.0 copy-done.4
  116.9 7.2 %compare_select_fusion = (bf16[2,800,800]{2,0,1:T(2,128)(2,1)S(1)}, bf16[2,800,800]{2,0,1:T(2,128)(2,1)S(1)}) fusion(bf16[16,2,50,800]{3,1,2,0:T(2,128)(2,1)S(1)} %copy.28, s32[800,800]{1,0:T(8,128)S(1)} %copy-done, s32[2]{0:T(128)S(1)} %copy-done.4, bf16[16,2,50,800]{3,1,2,0:T(2,128)(2,1)S(1)} %copy-done.1), kind=kLoop, calls=%fused_computation | loop fusion | flops 3840000 | bytes 12800008 | tf_op jit(solution)/shard_map/jit(_where)/select_n | solution.py:12
  124.1 4.8 fusion.6
  129.0 0.0 copy-start.3
  129.0 0.0 copy-start.5
  129.0 0.0 all-reduce.2.cloned.1.call-update
  129.0 0.7 copy-done.3
  129.7 0.0 copy-done.5
  129.7 0.1 broadcast_subtract_fusion
  129.7 9.6 %all-gather.3.cloned.1.call-done = bf16[16,50,800]{2,1,0:T(8,128)(2,1)} async-done(((bf16[1,50,800]{2,1,0:T(8,128)(2,1)}), bf16[16,50,800]{2,1,0:T(8,128)(2,1)}) %all-gather.3.cloned.1.call-update) | async-done | bytes 1280016 | tf_op jit(solution)/shard_map/all_gather | solution.py:27
  139.3 3.0 reshape.63
  142.4 254.5 %all-reduce.2.cloned.1.call-done = f32[800,800]{1,0:T(8,128)} async-done(((f32[800,800]{1,0:T(8,128)}), f32[800,800]{1,0:T(8,128)}) %all-reduce.2.cloned.1.call-update) | async-done | bytes 2560016 | tf_op jit(solution)/shard_map/psum | solution.py:26
  396.8 8.1 %fusion.4 = f32[2,800,800]{2,1,0:T(8,128)} fusion(bf16[2,800,800]{2,0,1:T(2,128)(2,1)S(1)} %get-tuple-element.6, f32[800,800]{1,0:T(8,128)} %all-reduce.2.cloned.1.call-done, f32[800,800]{1,0:T(8,128)} %reshape.63, s32[800]{0:T(1024)S(1)} %copy-done.2), kind=kOutput, calls=%fused_computation.8 | convolution fusion | flops 2050560000 | bytes 12803200 | tf_op jit(solution)/shard_map/pae,be->pab/dot_general | solution.py:32
  404.9 7.1 %copy.32 = f32[2,800,800]{1,2,0:T(8,128)} copy(f32[2,800,800]{2,1,0:T(8,128)} %fusion.4) | data formatting | bytes 10240000 | tf_op jit(solution)/shard_map/pae,be->pab/dot_general | solution.py:32
  412.0 5.1 fusion
  417.1 4.4 copy.33
  421.5 73.9 %all_to_all.54 = f32[2,800,800]{2,0,1:T(2,128)S(1)} all-to-all(f32[2,800,800]{2,0,1:T(2,128)S(1)} %copy.33), channel_id=1, replica_groups=mesh['grp'=16,'ing'=16] {'ing'}, dimensions={1} | all-to-all | bytes 10240000 | tf_op jit(solution)/shard_map/all_to_all | solution.py:37
  495.4 5.7 %copy.34 = f32[16,2,50,800]{3,1,0,2:T(2,128)} copy(f32[16,2,50,800]{3,1,2,0:T(2,128)S(1)} %bitcast.25) | data formatting | bytes 10240000 | tf_op jit(solution)/shard_map/all_to_all | solution.py:37
  501.1 7.8 %all_to_all.50 = f32[32,50,800]{2,0,1:T(8,128)} reshape(f32[16,2,50,800]{3,1,0,2:T(2,128)} %copy.34) | data formatting | bytes 10240000 | tf_op jit(solution)/shard_map/all_to_all | solution.py:37
Async XLA Ops:
  11.8 50.5 %all-to-all-start = ((bf16[32,50,800]{2,1,0:T(8,128)(2,1)}), bf16[32,50,800]{2,1,0:T(8,128)(2,1)S(1)}, u32[]{:S(2)}, u32[]{:S(2)}) async-start(bf16[32,50,800]{2,1,0:T(8,128)(2,1)} %copy.25), calls=%async_computation | async-start | bytes 6422528 | tf_op jit(solution)/shard_map/all_to_all | solution.py:18
  23.2 48.2 %copy-start.2 = (s32[800]{0:T(1024)S(1)}, s32[800]{0:T(1024)}, u32[]{:S(2)}) copy-start(s32[800]{0:T(1024)} %param.10) | copy-start | bytes 9604
  62.3 50.3 %all-to-all-start.1 = ((bf16[32,50,800]{2,1,0:T(8,128)(2,1)}), bf16[32,50,800]{2,1,0:T(8,128)(2,1)}, u32[]{:S(2)}, u32[]{:S(2)}) async-start(bf16[32,50,800]{2,1,0:T(8,128)(2,1)} %copy.27), calls=%async_computation.1 | async-start | bytes 6422528 | tf_op jit(solution)/shard_map/all_to_all | solution.py:19
  70.7 68.7 %all-gather.3.cloned.1.call-start = ((), (), s32[]{:S(2)}) async-start(), calls=%async_computation.4 | async-start | bytes 1705984 | tf_op jit(solution)/shard_map/all_gather | solution.py:27
  71.4 325.4 %all-reduce.2.cloned.1.call-start = ((), (), s32[]{:S(2)}) async-start(), calls=%async_computation.3 | async-start | bytes 5734400 | tf_op jit(solution)/shard_map/psum | solution.py:26
  112.6 4.3 copy-start
  112.6 4.3 copy-start.1
  112.6 4.3 copy-start.4
  129.0 0.7 copy-start.3
  129.0 0.7 copy-start.5
Sparse Core Ops, SparseCore 0:
  74.2 65.0 all-gather.2
Sparse Core Ops, SparseCore 1:
  129.1 267.7 all-reduce.1
where the time goes:
time: 517 us; the launch traced here: 516 us
  waiting for transfers between devices  339 us (66%)
  blocking collectives  73.9 us (14%)
  local copies, waits for them, and re-layouts  45.7 us (9%)
  starting transfers between devices  15.3 us (3%)
  between operations  14.9 us (3%)
  other arithmetic  14.3 us (3%)
  matrix products  12.9 us (2%)
    psum x1, waiting for transfers between devices, body(): correction = lax.psum(partial_value, ('grp', 'ing'))  254 us
    all_to_all x1, blocking collectives, body(): lax.all_to_all(scaled, 'ing', split_axis=1, concat_axis=0, tiled=True)  73.9 us
    all_to_all x1, waiting for transfers between devices, body(): lax.all_to_all(amplitudes, 'ing', split_axis=0, concat_axis=1, tiled=True)  39.1 us
    all_to_all x1, waiting for transfers between devices, body(): lax.all_to_all(integrals, 'ing', split_axis=0, concat_axis=1, tiled=True)  35.5 us
    all_to_all x2, local copies, waits for them, and re-layouts, body(): lax.all_to_all(scaled, 'ing', split_axis=1, concat_axis=0, tiled=True)  13.5 us
  transfers between devices with their start and end apart: 4, of which 4 were waited for; matrix products, arithmetic and copies ran while one was open for 6% of the time, Pallas kernels for 0%

commit v1 on v0

--- a/solution.py
+++ b/solution.py
@@ -1,7 +1,16 @@
+import functools
 import jax
 import jax.numpy as jnp
 from jax import lax
 from jax.sharding import PartitionSpec as P
+
+
+def balance_the_record(q_in, row_axis, a_name):
+    block_out = lax.psum(lax.psum(q_in, row_axis), a_name)
+    return block_out
+
+
+indices_get = functools.partial(balance_the_record, row_axis="grp", a_name="ing")
 
 
 def symmetry_mask(values, pair_irrep, virtual_irrep):
@@ -23,7 +32,7 @@
     partial_value = jnp.einsum(
         "paf,pef->ae", amp_masked, int_masked, preferred_element_type=jnp.float32
     )
-    correction = lax.psum(partial_value, ("grp", "ing"))
+    correction = indices_get(partial_value)
     fock_full = lax.all_gather(fock_block, "ing", axis=0, tiled=True)
     fock_part = jnp.where(
         same_irrep, fock_full.astype(jnp.float32), jnp.zeros(fock_full.shape, jnp.float32)

time: 517 us -> 474 us (0.917)
  waiting for transfers between devices: 339 us -> 295 us
    psum x1 -> x2, waiting for transfers between devices: 254 us -> 220 us  [balance_the_record(): block_out = lax.psum(lax.psum(q_in, row_axis), a_name)]
    all_gather x1, waiting for transfers between devices: 9.61 us -> 0.01 us  [body(): fock_full = lax.all_gather(fock_block, 'ing', axis=0, tiled=True)]
  transfers between devices with their start and end apart: 4 -> 5, of which waited for: 4 -> 4; matrix products, arithmetic and copies ran while one was open for 6% -> 3% of each run, Pallas kernels for 0% -> 0%
where the time goes in v1:
time: 474 us; the launch traced here: 470 us
  waiting for transfers between devices  295 us (62%)
  blocking collectives  71.9 us (15%)
  local copies, waits for them, and re-layouts  45.1 us (10%)
  starting transfers between devices  15.8 us (3%)
  between operations  14.9 us (3%)
  other arithmetic  14.1 us (3%)
  matrix products  12.9 us (3%)
    psum x2, waiting for transfers between devices, balance_the_record(): block_out = lax.psum(lax.psum(q_in, row_axis), a_name)  220 us
    all_to_all x1, blocking collectives, body(): lax.all_to_all(scaled, 'ing', split_axis=1, concat_axis=0, tiled=True)  71.9 us
    all_to_all x1, waiting for transfers between devices, body(): lax.all_to_all(amplitudes, 'ing', split_axis=0, concat_axis=1, tiled=True)  39.1 us
    all_to_all x1, waiting for transfers between devices, body(): lax.all_to_all(integrals, 'ing', split_axis=0, concat_axis=1, tiled=True)  35.2 us
    all_to_all x2, local copies, waits for them, and re-layouts, body(): lax.all_to_all(scaled, 'ing', split_axis=1, concat_axis=0, tiled=True)  13.5 us
  transfers between devices with their start and end apart: 5, of which 4 were waited for; matrix products, arithmetic and copies ran while one was open for 3% of the time, Pallas kernels for 0%

profile of v1, /device:TPU:99, one launch (start us, length us, event | category | flops | bytes accessed | tf_op | source)
XLA Modules:
  0.0 469.7 jit_solution(5832382185796731040)
XLA Ops:
  7.4 4.4 copy.25
  11.8 6.9 %all-to-all-start = ((bf16[32,50,800]{2,1,0:T(8,128)(2,1)}), bf16[32,50,800]{2,1,0:T(8,128)(2,1)S(1)}, u32[]{:S(2)}, u32[]{:S(2)}) async-start(bf16[32,50,800]{2,1,0:T(8,128)(2,1)} %copy.25), calls=%async_computation | async-start | bytes 6422528 | tf_op jit(solution)/shard_map/all_to_all | solution.py:27
  18.7 4.5 copy.27
  23.2 0.0 copy-start.2
  23.2 39.1 %all-to-all-done = bf16[32,50,800]{2,1,0:T(8,128)(2,1)S(1)} async-done(((bf16[32,50,800]{2,1,0:T(8,128)(2,1)}), bf16[32,50,800]{2,1,0:T(8,128)(2,1)S(1)}, u32[]{:S(2)}, u32[]{:S(2)}) %all-to-all-start) | async-done | bytes 2560032 | tf_op jit(solution)/shard_map/all_to_all | solution.py:27
  62.3 8.3 %all-to-all-start.1 = ((bf16[32,50,800]{2,1,0:T(8,128)(2,1)}), bf16[32,50,800]{2,1,0:T(8,128)(2,1)}, u32[]{:S(2)}, u32[]{:S(2)}) async-start(bf16[32,50,800]{2,1,0:T(8,128)(2,1)} %copy.27), calls=%async_computation.1 | async-start | bytes 6422528 | tf_op jit(solution)/shard_map/all_to_all | solution.py:28
  70.7 0.2 all-reduce.3.cloned.1.call-start
  70.9 0.0 copy-done.2
  70.9 1.8 broadcast_xor_fusion
  72.7 3.8 copy.26
  76.6 35.2 %all-to-all-done.1 = bf16[32,50,800]{2,1,0:T(8,128)(2,1)} async-done(((bf16[32,50,800]{2,1,0:T(8,128)(2,1)}), bf16[32,50,800]{2,1,0:T(8,128)(2,1)}, u32[]{:S(2)}, u32[]{:S(2)}) %all-to-all-start.1) | async-done | bytes 2560032 | tf_op jit(solution)/shard_map/all_to_all | solution.py:28
  111.8 0.0 copy-start
  111.8 0.0 copy-start.1
  111.8 0.0 copy-start.4
  111.8 4.3 copy.28
  116.1 0.0 copy-done
  116.1 0.0 copy-done.1
  116.1 0.0 copy-done.4
  116.1 7.0 %compare_select_fusion = (bf16[2,800,800]{2,0,1:T(2,128)(2,1)S(1)}, bf16[2,800,800]{2,0,1:T(2,128)(2,1)S(1)}) fusion(bf16[16,2,50,800]{3,1,2,0:T(2,128)(2,1)S(1)} %copy.28, s32[800,800]{1,0:T(8,128)S(1)} %copy-done, s32[2]{0:T(128)S(1)} %copy-done.4, bf16[16,2,50,800]{3,1,2,0:T(2,128)(2,1)S(1)} %copy-done.1), kind=kLoop, calls=%fused_computation | loop fusion | flops 3840000 | bytes 12800008 | tf_op jit(solution)/shard_map/jit(_where)/select_n | solution.py:21
  123.2 4.8 %fusion.6 = f32[800,800]{1,0:T(8,128)} fusion(bf16[2,800,800]{2,0,1:T(2,128)(2,1)S(1)} %get-tuple-element.5, bf16[2,800,800]{2,0,1:T(2,128)(2,1)S(1)} %get-tuple-element.6), kind=kOutput, calls=%fused_computation.10 | convolution fusion | flops 2048000000 | bytes 7680000 | tf_op jit(solution)/shard_map/paf,pef->ae/dot_general | solution.py:32
  128.0 0.0 copy-start.3
  128.0 0.0 copy-start.5
  128.0 0.0 all-reduce.3.cloned.1.call-update
  128.0 0.0 all-gather.3.cloned.1.call-start
  128.1 0.5 all-gather.3.cloned.1.call-update
  128.6 0.3 all-reduce.5.cloned.1.call-start
  128.9 121.1 %all-reduce.3.cloned.1.call-done = f32[800,800]{1,0:T(8,128)} async-done(((f32[800,800]{1,0:T(8,128)}), f32[800,800]{1,0:T(8,128)}) %all-reduce.3.cloned.1.call-update) | async-done | bytes 2560016 | tf_op jit(solution)/shard_map/psum | solution.py:9
  249.9 0.0 all-reduce.5.cloned.1.call-update
  249.9 0.0 copy-done.3
  249.9 0.0 copy-done.5
  250.0 0.1 broadcast_subtract_fusion
  250.0 0.0 all-gather.3.cloned.1.call-done
  250.0 3.0 reshape.63
  253.1 99.1 %all-reduce.5.cloned.1.call-done = f32[800,800]{1,0:T(8,128)} async-done(((f32[800,800]{1,0:T(8,128)}), f32[800,800]{1,0:T(8,128)}) %all-reduce.5.cloned.1.call-update) | async-done | bytes 2560016 | tf_op jit(solution)/shard_map/psum | solution.py:9
  352.1 8.1 %fusion.4 = f32[2,800,800]{2,1,0:T(8,128)} fusion(bf16[2,800,800]{2,0,1:T(2,128)(2,1)S(1)} %get-tuple-element.6, f32[800,800]{1,0:T(8,128)} %all-reduce.5.cloned.1.call-done, f32[800,800]{1,0:T(8,128)} %reshape.63, s32[800]{0:T(1024)S(1)} %copy-done.2), kind=kOutput, calls=%fused_computation.8 | convolution fusion | flops 2050560000 | bytes 12803200 | tf_op jit(solution)/shard_map/pae,be->pab/dot_general | solution.py:41
  360.2 7.1 %copy.32 = f32[2,800,800]{1,2,0:T(8,128)} copy(f32[2,800,800]{2,1,0:T(8,128)} %fusion.4) | data formatting | bytes 10240000 | tf_op jit(solution)/shard_map/pae,be->pab/dot_general | solution.py:41
  367.3 5.1 %fusion = f32[2,800,800]{2,1,0:T(8,128)S(1)} fusion(f32[2,800,800]{2,1,0:T(8,128)} %fusion.4, f32[2,800,800]{1,2,0:T(8,128)} %copy.32, f32[800]{0:T(1024)S(1)} %copy-done.3, f32[2,800]{1,0:T(2,128)S(1)} %broadcast_subtract_fusion), kind=kLoop, calls=%fused_computation.3 | loop fusion | flops 3840000 | bytes 15369600 | tf_op jit(solution)/shard_map/div | solution.py:45
  372.4 4.4 copy.33
  376.9 71.9 %all_to_all.54 = f32[2,800,800]{2,0,1:T(2,128)S(1)} all-to-all(f32[2,800,800]{2,0,1:T(2,128)S(1)} %copy.33), channel_id=1, replica_groups=mesh['grp'=16,'ing'=16] {'ing'}, dimensions={1} | all-to-all | bytes 10240000 | tf_op jit(solution)/shard_map/all_to_all | solution.py:46
  448.7 5.7 %copy.34 = f32[16,2,50,800]{3,1,0,2:T(2,128)} copy(f32[16,2,50,800]{3,1,2,0:T(2,128)S(1)} %bitcast.25) | data formatting | bytes 10240000 | tf_op jit(solution)/shard_map/all_to_all | solution.py:46
  454.4 7.8 %all_to_all.50 = f32[32,50,800]{2,0,1:T(8,128)} reshape(f32[16,2,50,800]{3,1,0,2:T(2,128)} %copy.34) | data formatting | bytes 10240000 | tf_op jit(solution)/shard_map/all_to_all | solution.py:46
Async XLA Ops:
  11.8 50.5 %all-to-all-start = ((bf16[32,50,800]{2,1,0:T(8,128)(2,1)}), bf16[32,50,800]{2,1,0:T(8,128)(2,1)S(1)}, u32[]{:S(2)}, u32[]{:S(2)}) async-start(bf16[32,50,800]{2,1,0:T(8,128)(2,1)} %copy.25), calls=%async_computation | async-start | bytes 6422528 | tf_op jit(solution)/shard_map/all_to_all | solution.py:27
  23.2 47.7 %copy-start.2 = (s32[800]{0:T(1024)S(1)}, s32[800]{0:T(1024)}, u32[]{:S(2)}) copy-start(s32[800]{0:T(1024)} %param.10) | copy-start | bytes 9604
  62.3 49.5 %all-to-all-start.1 = ((bf16[32,50,800]{2,1,0:T(8,128)(2,1)}), bf16[32,50,800]{2,1,0:T(8,128)(2,1)}, u32[]{:S(2)}, u32[]{:S(2)}) async-start(bf16[32,50,800]{2,1,0:T(8,128)(2,1)} %copy.27), calls=%async_computation.1 | async-start | bytes 6422528 | tf_op jit(solution)/shard_map/all_to_all | solution.py:28
  70.7 179.3 %all-reduce.3.cloned.1.call-start = ((), (), s32[]{:S(2)}) async-start(), calls=%async_computation.3 | async-start | bytes 5734400 | tf_op jit(solution)/shard_map/psum | solution.py:9
  111.8 4.3 copy-start
  111.8 4.3 copy-start.1
  111.8 4.3 copy-start.4
  128.0 122.0 %copy-start.3 = (f32[800]{0:T(1024)S(1)}, f32[800]{0:T(1024)}, u32[]{:S(2)}) copy-start(f32[800]{0:T(1024)} %param.13) | copy-start | bytes 9604
  128.0 122.0 %copy-start.5 = (f32[2]{0:T(128)S(1)}, f32[2]{0:T(128)}, u32[]{:S(2)}) copy-start(f32[2]{0:T(128)} %param.12) | copy-start | bytes 28
  128.0 122.0 %all-gather.3.cloned.1.call-start = ((), (), s32[]{:S(2)}) async-start(), calls=%async_computation.5 | async-start | bytes 1705984 | tf_op jit(solution)/shard_map/all_gather | solution.py:36
  128.6 223.6 %all-reduce.5.cloned.1.call-start = ((), (), s32[]{:S(2)}) async-start(), calls=%async_computation.4 | async-start | bytes 5734400 | tf_op jit(solution)/shard_map/psum | solution.py:9
Sparse Core Ops, SparseCore 0:
  128.1 121.7 all-reduce.2
Sparse Core Ops, SparseCore 1:
  130.9 51.1 all-gather.2
  250.0 102.1 all-reduce.4
